TPU v7x, 32 devices: a whole 2x2x4 slice. The times are simulated.
32 devices in a mesh: blk: 2 (over x), wide: 16 (over z, y, core).
Axes of the slice: x: 2, y: 2, z: 4, core: 2. Of those that a mesh axis runs over, the one named last changes fastest.
Arguments:
- resid: bfloat16 [8192, 1024], P('wide', 'blk'), may hold values from -24 to 24
- samples: bfloat16 [8192, 1024], P('wide', 'blk'), may hold values from -6 to 6
- precision: float32 [64, 2, 32, 128, 128], P('wide', 'blk'), as said below
- active: int32 [64, 2, 32], P('wide', 'blk'), may hold values 0 or 1
Outputs:
- updated: float32 [64, 2, 32, 128, 128], P('wide', 'blk')
Inputs may be any that keep to these rules, and one draw needn't show every extreme that they name: `precision`: entries on the diagonal of W lie between 1 and 2.
All inputs are finite; a program needn't handle non-finite values. No bound on the sum of `active` on one device may be relied on, other than what follows from the above.
Results may differ from a plain program's by a relative error of at most 0.0003.
Values may be sent and summed in bfloat16 or wider, within the bound.
A program may use at most 192 MiB of HBM per device.

v0:
```python
import jax
import jax.numpy as jnp
from jax import lax
from jax.sharding import PartitionSpec as P

STEP = 1.0
LASSO = 0.1
RIDGE = 0.5


def local(resid, samples, precision, active):
    groups = lax.axis_size("blk")
    column_group = lax.axis_index("blk")
    panel_index = lax.axis_index("wide")
    row_tiles = precision.shape[0]
    per_class = precision.shape[2]
    tile_size = precision.shape[3]
    tiles = per_class * groups
    local_samples = resid.shape[1]
    total_samples = local_samples * groups
    own_rows = panel_index * row_tiles + jnp.arange(row_tiles, dtype=jnp.int32)
    first_column = (column_group - own_rows) % groups
    own_resid = resid.reshape(row_tiles, tile_size, local_samples)
    own_data = samples.reshape(row_tiles, tile_size, local_samples)
    all_resid, all_data = (
        lax.all_gather(resid, "wide", axis=0, tiled=True),
        lax.all_gather(samples, "wide", axis=0, tiled=True),
    )
    resid_tiles = all_resid.reshape(tiles, tile_size, local_samples)
    data_tiles = all_data.reshape(tiles, tile_size, local_samples)
    positions = jnp.arange(per_class * lax.axis_size("blk"), dtype=jnp.int32)
    classes = positions // per_class
    within = positions % per_class
    column_ids = (classes[:, None] - own_rows[None, :]) % groups + groups * within[:, None]
    forward = jnp.einsum(
        "kis,pkjs->pkij", own_resid, data_tiles[column_ids], preferred_element_type=jnp.float32
    )
    backward = jnp.einsum(
        "kis,pkjs->pkij", own_data, resid_tiles[column_ids], preferred_element_type=jnp.float32
    )
    summed = (
        lax.psum_scatter(0.5 * (forward + backward), "blk", scatter_dimension=0, tiled=True)
        / total_samples
    )
    precision_tiles = precision[:, 0]
    active_flags = active[:, 0].astype(jnp.float32)
    gradient_part = summed.transpose(1, 0, 2, 3)
    column_ids = first_column[:, None] + groups * jnp.arange(per_class, dtype=jnp.int32)[None, :]
    same_tile = column_ids == own_rows[:, None]
    identity = jnp.eye(tile_size, dtype=bool)
    on_diag = same_tile[:, :, None, None] & identity
    inverse = jnp.where(on_diag, 1.0 / jnp.where(on_diag, precision_tiles, 1.0), 0.0)
    stepped = precision_tiles - STEP * (gradient_part + RIDGE * precision_tiles - inverse)
    shrunk = jnp.sign(stepped) * jnp.maximum(jnp.abs(stepped) - STEP * LASSO, 0.0)
    updated = jnp.where(on_diag, stepped, shrunk) * active_flags[:, :, None, None]
    return updated[:, None]


def solution(mesh):
    in_specs = (
        P("wide", "blk"),
        P("wide", "blk"),
        P("wide", "blk", None, None, None),
        P("wide", "blk", None),
    )
    out_specs = P("wide", "blk", None, None, None)
    return jax.shard_map(local, mesh=mesh, in_specs=in_specs, out_specs=out_specs, check_vma=False)
```

profile of v0, /device:TPU:0, one launch (start us, length us, event | category | flops | bytes accessed | tf_op | source)
XLA Modules:
  0.0 459.7 jit_solution(1538638728319568787)
XLA Ops:
  6.5 0.0 all-gather.5.cloned.1.call-start
  6.5 0.7 all-gather.5.cloned.1.call-update
  7.3 0.0 all-gather.3.cloned.1.call-start
  7.3 0.7 all-gather.3.cloned.1.call-update
  8.0 0.0 reduce-scatter.5.cloned.1.call-start
  8.1 0.1 compare_select_fusion
  8.2 0.1 reshape.233
  8.3 78.3 %all-gather.5.cloned.1.call-done = bf16[8192,512]{1,0:T(8,128)(2,1)} async-done(((bf16[512,512]{1,0:T(8,128)(2,1)}), bf16[8192,512]{1,0:T(8,128)(2,1)}) %all-gather.5.cloned.1.call-update) | async-done | bytes 8388624 | tf_op jit(solution)/shard_map/all_gather | solution.py:26
  86.5 17.5 %gather_fusion.1 = bf16[256,128,512]{2,1,0:T(8,128)(2,1)} fusion(bf16[64,128,512]{2,1,0:T(8,128)(2,1)} %bitcast.53, s32[1024]{0:T(1024)S(1)} %pad_clamp_fusion), kind=kCustom, calls=%fused_computation.1 | custom fusion | bytes 67109888 | tf_op jit(solution)/shard_map/gather | solution.py:39
  104.0 57.6 %all-gather.3.cloned.1.call-done = bf16[8192,512]{1,0:T(8,128)(2,1)} async-done(((bf16[512,512]{1,0:T(8,128)(2,1)}), bf16[8192,512]{1,0:T(8,128)(2,1)}) %all-gather.3.cloned.1.call-update) | async-done | bytes 8388624 | tf_op jit(solution)/shard_map/all_gather | solution.py:27
  161.6 0.0 copy-start.2
  161.6 17.3 %gather_fusion = bf16[256,128,512]{2,1,0:T(8,128)(2,1)} fusion(bf16[64,128,512]{2,1,0:T(8,128)(2,1)} %bitcast.54, s32[1024]{0:T(1024)S(1)} %pad_clamp_fusion), kind=kCustom, calls=%fused_computation | custom fusion | bytes 67109888 | tf_op jit(solution)/shard_map/gather | solution.py:36
  179.0 0.0 copy-done.2
  179.0 0.0 copy-start.1
  179.0 21.1 %fusion = f32[4,64,128,128]{3,2,1,0:T(8,128)} fusion(bf16[4,128,512,1]{2,1,3,0:T(8,128)(2,1)S(1)} %bitcast.61, bf16[64,4,128,512]{3,2,1,0:T(8,128)(2,1)} %bitcast.58), kind=kOutput, calls=%fused_computation.2 | convolution fusion | flops 4294967296 | bytes 50855936 | tf_op jit(solution)/shard_map/kis,pkjs->pkij/dot_general | solution.py:38
  200.1 0.0 copy-done.1
  200.1 24.1 %multiply_bitcast_fusion = f32[64,4,128,128]{2,3,0,1:T(8,128)} fusion(f32[4,64,128,128]{3,2,1,0:T(8,128)} %fusion, bf16[4,128,512,1]{2,1,3,0:T(8,128)(2,1)S(1)} %bitcast.60, bf16[64,4,128,512]{3,2,1,0:T(8,128)(2,1)} %bitcast.52), kind=kOutput, calls=%fused_computation.7 | convolution fusion | flops 4303355904 | bytes 67633152 | tf_op jit(solution)/shard_map/kis,pkjs->pkij/dot_general | solution.py:35
  224.2 6.5 %copy.17 = f32[64,4,128,128]{2,3,1,0:T(8,128)S(1)} copy(f32[64,4,128,128]{2,3,0,1:T(8,128)} %multiply_bitcast_fusion) | data formatting | bytes 33554432
  230.7 11.7 %copy.37 = f32[8,8,512,128]{3,1,2,0:T(8,128)} copy(f32[8,8,512,128]{3,2,1,0:T(8,128)S(1)} %bitcast.56) | data formatting | bytes 33554432
  242.5 0.0 reduce-scatter.5.cloned.1.call-update
  242.5 0.0 copy-start.3
  242.5 9.0 %copy.11 = f32[4,1,32,128,128]{3,4,2,0,1:T(8,128)} copy(f32[4,1,32,128,128]{4,3,2,1,0:T(8,128)} %param.6) | data formatting | bytes 16777216 | tf_op args[2]
  251.5 0.0 copy-done.3
  251.5 0.1 add_compare_fusion
  251.6 178.8 %reduce-scatter.5.cloned.1.call-done = f32[32,65536]{1,0:T(8,128)} async-done(((f32[64,65536]{1,0:T(8,128)}), f32[32,65536]{1,0:T(8,128)}) %reduce-scatter.5.cloned.1.call-update) | async-done | bytes 8388624
  430.4 0.0 copy-start
  430.4 5.0 %copy.20 = f32[4,8,512,128]{3,2,1,0:T(8,128)S(1)} copy(f32[4,8,512,128]{3,1,2,0:T(8,128)} %bitcast.59) | data formatting | bytes 16777216
  435.5 0.7 copy-done
  436.2 8.0 %fusion.10 = f32[4,1,32,128,128]{3,4,2,0,1:T(8,128)} fusion(f32[32,4,128,128]{2,3,1,0:T(8,128)S(1)} %bitcast.57, f32[4,1,32,128,128]{3,4,2,0,1:T(8,128)S(1)} %copy-done, f32[4,32]{1,0:T(4,128)S(1)} %bitcast.62, pred[128,128]{0,1:T(8,128)(4,1)S(1)} %iota_compare_fusion, pred[4,32]{1,0:T(4,128)(4,1)S(1)} %add_compare_fusion), kind=kLoop, calls=%fused_computation.15 | loop fusion | flops 33554432 | bytes 25182848 | tf_op jit(solution)/shard_map/broadcast_in_dim | solution.py:56
  444.2 8.9 %copy.14 = f32[4,1,32,128,128]{4,3,2,1,0:T(8,128)} copy(f32[4,1,32,128,128]{3,4,2,0,1:T(8,128)} %fusion.10) | data formatting | bytes 16777216 | tf_op jit(solution)/shard_map/broadcast_in_dim | solution.py:56
  (7 shorter events, 0.0 us)
Async XLA Ops:
  6.5 80.0 %all-gather.5.cloned.1.call-start = ((), (), s32[]{:S(2)}) async-start(), calls=%async_computation.2 | async-start | bytes 8912896 | tf_op jit(solution)/shard_map/all_gather | solution.py:26
  7.3 154.4 %all-gather.3.cloned.1.call-start = ((), (), s32[]{:S(2)}) async-start(), calls=%async_computation.1 | async-start | bytes 8912896 | tf_op jit(solution)/shard_map/all_gather | solution.py:27
  8.0 422.4 %reduce-scatter.5.cloned.1.call-start = ((), (), s32[]{:S(2)}) async-start(), calls=%async_computation.3 | async-start | bytes 25165824
  161.6 17.4 %copy-start.2 = (bf16[512,512]{1,0:T(8,128)(2,1)S(1)}, bf16[512,512]{1,0:T(8,128)(2,1)}, u32[]{:S(2)}) copy-start(bf16[512,512]{1,0:T(8,128)(2,1)} %param.5) | copy-start | bytes 1572868
  179.0 21.1 %copy-start.1 = (bf16[512,512]{1,0:T(8,128)(2,1)S(1)}, bf16[512,512]{1,0:T(8,128)(2,1)}, u32[]{:S(2)}) copy-start(bf16[512,512]{1,0:T(8,128)(2,1)} %param.4) | copy-start | bytes 1572868
  242.5 9.0 %copy-start.3 = (s32[4,1,32]{2,1,0:T(1,128)S(1)}, s32[4,1,32]{2,1,0:T(1,128)}, u32[]{:S(2)}) copy-start(s32[4,1,32]{2,1,0:T(1,128)} %param.7) | copy-start | bytes 1540
  430.4 5.8 %copy-start = (f32[4,1,32,128,128]{3,4,2,0,1:T(8,128)S(1)}, f32[4,1,32,128,128]{3,4,2,0,1:T(8,128)}, u32[]{:S(2)}) copy-start(f32[4,1,32,128,128]{3,4,2,0,1:T(8,128)} %copy.11) | copy-start | bytes 25165828
Sparse Core Ops, SparseCore 0:
  9.5 77.0 all-gather.4
  88.7 72.8 all-gather.2
  242.6 187.7 reduce-scatter.4
where the time goes:
time: 460 us
  waiting for transfers between devices  316 us (69%)
  local copies, waits for them, and re-layouts  76.9 us (17%)
  matrix products  45.2 us (10%)
  between operations  13.2 us (3%)
  other arithmetic  8.24 us (2%)
    unnamed x4, waiting for transfers between devices  180 us
    all_gather x1, waiting for transfers between devices, local(): lax.all_gather(resid, 'wide', axis=0, tiled=True)  78.3 us
    all_gather x1, waiting for transfers between devices, local(): lax.all_gather(samples, 'wide', axis=0, tiled=True)  57.6 us
    unnamed x12, local copies, waits for them, and re-layouts  33 us
    dot_general x1, matrix products, local(): jnp.einsum('kis,pkjs->pkij', own_resid, data_tiles[column_ids], preferred...  24.1 us
    dot_general x1, matrix products, local(): jnp.einsum('kis,pkjs->pkij', own_data, resid_tiles[column_ids], preferred...  21.1 us
    gather x1, local copies, waits for them, and re-layouts, local(): resid_tiles[column_ids]  17.5 us
    gather x1, local copies, waits for them, and re-layouts, local(): data_tiles[column_ids]  17.3 us
  transfers between devices with their start and end apart: 3, of which 3 were waited for; matrix products, arithmetic and copies ran while one was open for 6% of the time, Pallas kernels for 0%

commit v1 on v0

--- a/solution.py
+++ b/solution.py
@@ -1,6 +1,10 @@
+import functools
+
 import jax
 import jax.numpy as jnp
 from jax import lax
+from jax.experimental import pallas as pl
+from jax.experimental.pallas import tpu as pltpu
 from jax.sharding import PartitionSpec as P
 
 STEP = 1.0
@@ -56,6 +60,317 @@
     return updated[:, None]
 
 
+MESH = pl.DeviceIdType.MESH
+
+
+def pick(table, i):
+    value = jnp.int32(table[0])
+    for n in range(1, len(table)):
+        value = jnp.where(i == n, jnp.int32(table[n]), value)
+    return value
+
+
+def kernel(
+    depth, scale, resid, samples, weights, flags, out,
+    own, cols, held, stage, landed, recv, own_recv, res_recv, send, res_send, fill, out_sem,
+):
+    b = lax.axis_index("blk")
+    w = lax.axis_index("wide")
+    nb = 1 - b
+    z, y, c = w // 4, (w // 2) % 2, w % 2
+    per = own.shape[3]
+    tile = own.shape[4]
+    panels = cols.shape[1]
+    up, down = (z + 1 < depth), (z > 0)
+
+    def at(zz, yy, cc):
+        return (zz * 2 + yy) * 2 + cc
+
+    orders = [sorted((o for o in range(depth) if o != i), key=lambda o: (abs(o - i), o)) for i in range(depth)]
+
+    def order(k):
+        value = z
+        for n in range(1, depth):
+            value = jnp.where(k == n, pick([orders[i][n - 1] for i in range(depth)], z), value)
+        return value
+
+    loads = []
+    for a, src in enumerate((resid, samples)):
+        for p in range(2):
+            loads.append(pltpu.make_async_copy(src.at[:, p], own.at[b, p, a], fill.at[2 * a + p]))
+    for load in loads:
+        load.start()
+    load_weights = pltpu.make_async_copy(weights, held, fill.at[4])
+    load_weights.start()
+
+    barrier = pltpu.get_barrier_semaphore()
+
+    def greet(**device):
+        pl.semaphore_signal(barrier, inc=1, device_id=device, device_id_type=MESH)
+
+    greet(blk=nb)
+    greet(wide=at(z, 1 - y, c))
+    greet(wide=at(z, y, 1 - c))
+
+    @pl.when(up)
+    def _():
+        greet(wide=at(z + 1, y, c))
+
+    @pl.when(down)
+    def _():
+        greet(wide=at(z - 1, y, c))
+
+    pl.semaphore_wait(barrier, 3 + jnp.where(up, 1, 0) + jnp.where(down, 1, 0))
+
+    def push(h, src, panel, k, lane, target):
+        return pltpu.make_async_remote_copy(
+            src_ref=src, dst_ref=cols.at[h, panel], send_sem=send.at[h, k, lane],
+            recv_sem=recv.at[h, panel], device_id={"wide": target}, device_id_type=MESH,
+        )
+
+    def arrive(h, panel):
+        push(h, cols.at[h, panel], panel, 0, 0, at(z, 1 - y, c)).wait_recv()
+
+    def own_pushes(h):
+        src = own.at[h, b]
+        return (
+            (up, push(h, src, w, 0, 0, at(z + 1, y, c))),
+            (down, push(h, src, w, 0, 1, at(z - 1, y, c))),
+            (None, push(h, src, w, 0, 2, at(z, 1 - y, c))),
+            (None, push(h, src, w, 0, 3, at(z, y, 1 - c))),
+        )
+
+    def z_pushes(h, k):
+        zk = order(k)
+        panel = at(zk, y, c)
+        src = cols.at[h, panel]
+        onward = jnp.where(zk < z, z + 1, z - 1)
+        exists = jnp.logical_and(onward >= 0, onward < depth)
+        return (
+            (exists, push(h, src, panel, k, 0, at(onward, y, c))),
+            (None, push(h, src, panel, k, 2, at(z, 1 - y, c))),
+            (None, push(h, src, panel, k, 3, at(z, y, 1 - c))),
+        )
+
+    def y_push(h, k):
+        panel = at(order(k), 1 - y, c)
+        return ((None, push(h, cols.at[h, panel], panel, k, 4, at(z, y, 1 - c))),)
+
+    def start(pushes):
+        for when, copy in pushes:
+            if when is None:
+                copy.start()
+            else:
+                pl.when(when)(copy.start)
+
+    def drain(pushes):
+        for when, copy in pushes:
+            if when is None:
+                copy.wait_send()
+            else:
+                pl.when(when)(copy.wait_send)
+
+    def forward_z(k):
+        for h in (b, nb):
+            arrive(h, at(order(k), y, c))
+            start(z_pushes(h, k))
+
+    def swap(i):
+        p = nb if i == 0 else b
+        return pltpu.make_async_remote_copy(
+            src_ref=own.at[b, p], dst_ref=own.at[b, p], send_sem=res_send.at[panels + i],
+            recv_sem=own_recv.at[i], device_id={"blk": nb}, device_id_type=MESH,
+        )
+
+    def hand(panel):
+        return pltpu.make_async_remote_copy(
+            src_ref=stage.at[panel], dst_ref=landed.at[panel], send_sem=res_send.at[panel],
+            recv_sem=res_recv.at[panel], device_id={"blk": nb}, device_id_type=MESH,
+        )
+
+    def store(p, panel):
+        span = pl.ds(panel * per, per)
+        return pltpu.make_async_copy(
+            held.at[:, p, span], out.at[:, p, span], out_sem.at[p, panel]
+        )
+
+    def gram(p, side):
+        total = None
+        for h in range(2):
+            for a in range(2):
+                left = own[h, p, a].reshape(per * tile, -1)
+                right = side(h, 1 - a).reshape(per * tile, -1)
+                part = lax.dot_general(
+                    left, right, (((1,), (1,)), ((), ())), preferred_element_type=jnp.float32
+                )
+                total = part if total is None else total + part
+        return total * scale
+
+    def finish(p, panel, part, diagonal):
+        for t in range(per):
+            for u in range(per):
+                slot = panel * per + u
+                weight = held[t, p, slot]
+                half = part(t, u) + RIDGE * weight
+                if diagonal and t == u:
+                    rows = lax.broadcasted_iota(jnp.int32, (tile, tile), 0)
+                    columns = lax.broadcasted_iota(jnp.int32, (tile, tile), 1)
+                    on_diag = rows == columns + b * (2 * tile)
+                    inverse = jnp.where(on_diag, 1.0 / jnp.where(on_diag, weight, 1.0), 0.0)
+                    stepped = weight - STEP * (half - inverse)
+                else:
+                    stepped = weight - STEP * half
+                bound = STEP * LASSO
+                updated = stepped - jnp.clip(stepped, -bound, bound)
+                if diagonal and t == u:
+                    updated = jnp.where(on_diag, stepped, updated)
+                flag = flags[2 * t + p, slot].astype(jnp.float32)
+                held[t, p, slot] = updated * flag
+        store(p, panel).start()
+
+    for load in loads:
+        load.wait()
+    for i in range(2):
+        swap(i).start()
+    start(own_pushes(b))
+    swap_in = [
+        pltpu.make_async_remote_copy(
+            src_ref=own.at[nb, p], dst_ref=own.at[nb, p], send_sem=res_send.at[panels + i],
+            recv_sem=own_recv.at[i], device_id={"blk": nb}, device_id_type=MESH,
+        )
+        for i, p in enumerate((b, nb))
+    ]
+    swap_in[0].wait_recv()
+    start(own_pushes(nb))
+    swap_in[1].wait_recv()
+    forward_z(1)
+    load_weights.wait()
+
+    for p in range(2):
+        parity = b if p == 0 else nb
+        total = gram(p, lambda h, a: own[h, parity, a])
+        finish(p, w, lambda t, u: total[t * tile:(t + 1) * tile, u * tile:(u + 1) * tile], True)
+
+    def place(s):
+        k, i = s // 4, s % 4
+        yy = jnp.where(i < 2, y, 1 - y)
+        cc = jnp.where(i % 2 == 0, c, 1 - c)
+        return k, i, at(order(k), yy, cc)
+
+    def compute(s, carry):
+        k, i, panel = place(s)
+
+        @pl.when(jnp.logical_and(i == 2, jnp.logical_and(k > 0, k < depth - 1)))
+        def _():
+            forward_z(k + 1)
+
+        @pl.when(i != 0)
+        def _():
+            for h in (b, nb):
+                arrive(h, panel)
+
+        @pl.when(i == 2)
+        def _():
+            for h in (b, nb):
+                start(y_push(h, k))
+
+        total = gram(1, lambda h, a: cols[h, panel, a])
+        for t in range(per):
+            for u in range(per):
+                stage[panel, t, u] = total[t * tile:(t + 1) * tile, u * tile:(u + 1) * tile]
+        hand(panel).start()
+        kept = gram(0, lambda h, a: cols[h, panel, a])
+        finish(0, panel, lambda t, u: kept[t * tile:(t + 1) * tile, u * tile:(u + 1) * tile], False)
+        return carry
+
+    lax.fori_loop(1, 4 * depth, compute, 0)
+
+    def receive(s, carry):
+        panel = place(s)[2]
+        hand(panel).wait_recv()
+        finish(1, panel, lambda t, u: landed[panel, t, u], False)
+        return carry
+
+    lax.fori_loop(1, 4 * depth, receive, 0)
+
+    for i in range(2):
+        swap(i).wait_send()
+    for h in (b, nb):
+        drain(own_pushes(h))
+
+    def drain_group(k, carry):
+        for h in (b, nb):
+            drain(y_push(h, k))
+
+            @pl.when(k > 0)
+            def _():
+                drain(z_pushes(h, k))
+        return carry
+
+    lax.fori_loop(0, depth, drain_group, 0)
+
+    def drain_panel(s, carry):
+        panel = place(s)[2]
+        hand(panel).wait_send()
+        for p in range(2):
+            store(p, panel).wait()
+        return carry
+
+    lax.fori_loop(1, 4 * depth, drain_panel, 0)
+    for p in range(2):
+        store(p, w).wait()
+
+
+def ring(resid, samples, precision, active):
+    panels = lax.axis_size("wide")
+    row_tiles, _, per_class, tile, _ = precision.shape
+    per = row_tiles // 2
+    half = resid.shape[1]
+    depth = panels // 4
+    scale = 0.5 / (2 * half)
+    any_spec = pl.BlockSpec(memory_space=pl.ANY)
+    bf16, f32 = resid.dtype, jnp.float32
+    dma = pltpu.SemaphoreType.DMA
+    updated = pl.pallas_call(
+        functools.partial(kernel, depth, scale),
+        out_shape=jax.ShapeDtypeStruct((per, 2, per_class, tile, tile), f32),
+        in_specs=[any_spec, any_spec, any_spec, pl.BlockSpec(memory_space=pltpu.SMEM)],
+        out_specs=any_spec,
+        scratch_shapes=[
+            pltpu.VMEM((2, 2, 2, per, tile, half), bf16),
+            pltpu.VMEM((2, panels, 2, per, tile, half), bf16),
+            pltpu.VMEM((per, 2, per_class, tile, tile), f32),
+            pltpu.VMEM((panels, per, per, tile, tile), f32),
+            pltpu.VMEM((panels, per, per, tile, tile), f32),
+            dma((2, panels)),
+            dma((2,)),
+            dma((panels,)),
+            dma((2, depth, 5)),
+            dma((panels + 2,)),
+            dma((5,)),
+            dma((2, panels)),
+        ],
+        compiler_params=pltpu.CompilerParams(
+            collective_id=0, has_side_effects=True, vmem_limit_bytes=60 * 1024 * 1024
+        ),
+    )(
+        resid.reshape(per, 2, tile, half),
+        samples.reshape(per, 2, tile, half),
+        precision.reshape(per, 2, per_class, tile, tile),
+        active[:, 0],
+    )
+    return updated.reshape(precision.shape)
+
+
+def body(resid, samples, precision, active):
+    panels = lax.axis_size("wide")
+    row_tiles, _, per_class, tile, _ = precision.shape
+    words = 8 * per_class * row_tiles * tile * tile + 4 * panels * row_tiles * tile * resid.shape[1]
+    if lax.axis_size("blk") == 2 and panels % 4 == 0 and row_tiles % 2 == 0 and words < 52 * 1024 * 1024:
+        return ring(resid, samples, precision, active)
+    return local(resid, samples, precision, active)
+
+
 def solution(mesh):
     in_specs = (
         P("wide", "blk"),
@@ -64,4 +379,4 @@
         P("wide", "blk", None),
     )
     out_specs = P("wide", "blk", None, None, None)
-    return jax.shard_map(local, mesh=mesh, in_specs=in_specs, out_specs=out_specs, check_vma=False)
+    return jax.shard_map(body, mesh=mesh, in_specs=in_specs, out_specs=out_specs, check_vma=False)

time: 460 us -> 131 us (0.28)
  waiting for transfers between devices: 316 us -> 0 us
  Pallas kernels: 0 us -> 123 us
  local copies, waits for them, and re-layouts: 76.9 us -> 7.89 us
  matrix products: 45.2 us -> 0 us
  between operations: 13.2 us -> 0.01 us
  other arithmetic: 8.24 us -> 0 us
    unnamed x4 -> x0, waiting for transfers between devices: 180 us -> none
    all_gather x2 -> x0, waiting for transfers between devices: 136 us -> none  [the longest x1 78.3 us: local(): lax.all_gather(resid, 'wide', axis=0, tiled=True)]
    pallas_call x0 -> x1, Pallas kernels: none -> 123 us  [ring(): pl.pallas_call(functools.partial(kernel, depth, scale), out_shape=jax.Sha...]
    dot_general x2 -> x0, matrix products: 45.2 us -> none  [the longest x1 24.1 us: local(): jnp.einsum('kis,pkjs->pkij', own_resid, data_tiles[column_ids], preferred...]
    gather x2 -> x0, local copies, waits for them, and re-layouts: 34.8 us -> none  [the longest x1 17.5 us: local(): resid_tiles[column_ids]]
    unnamed x12 -> x1, local copies, waits for them, and re-layouts: 33 us -> 7.89 us
    broadcast_in_dim x1 -> x0, local copies, waits for them, and re-layouts: 8.93 us -> none  [local(): return updated[:, None]]
    broadcast_in_dim x1 -> x0, other arithmetic: 8.02 us -> none  [local(): return updated[:, None]]
  transfers between devices with their start and end apart: 3 -> 0, of which waited for: 3 -> 0; matrix products, arithmetic and copies ran while one was open for 6% -> 0% of each run, Pallas kernels for 0% -> 0%
where the time goes in v1:
time: 131 us
  Pallas kernels  123 us (94%)
  local copies, waits for them, and re-layouts  7.89 us (6%)
    pallas_call x1, Pallas kernels, ring(): pl.pallas_call(functools.partial(kernel, depth, scale), out_shape=jax.Sha...  123 us
    unnamed x1, local copies, waits for them, and re-layouts  7.89 us

profile of v1, /device:TPU:0, one launch (start us, length us, event | category | flops | bytes accessed | tf_op | source)
XLA Modules:
  0.0 131.2 jit_solution(3441430791064748517)
XLA Ops:
  0.0 123.3 %shard_map.46 = f32[2,2,32,128,128]{4,3,2,1,0:T(8,128)} custom-call(bf16[2,2,128,512]{3,2,1,0:T(8,128)(2,1)} %bitcast.9, bf16[2,2,128,512]{3,2,1,0:T(8,128)(2,1)} %bitcast.10, f32[2,2,32,128,128]{4,3,2,1,0:T(8,128)} %bitcast.8, s32[4,32]{1,0:T(4,128)} %bitcast.11), custom_call_target="tpu_custom_call" | custom-call | tf_op jit(solution)/shard_map/pallas_call | solution.py:334
  123.3 7.9 %copy.7 = f32[4,1,32,128,128]{4,3,2,1,0:T(8,128)} copy(f32[4,1,32,128,128]{4,3,2,1,0:T(8,128)} %bitcast.7) | data formatting | bytes 16777216

commit v2 on v1

--- a/solution.py
+++ b/solution.py
@@ -71,8 +71,8 @@
 
 
 def kernel(
-    depth, scale, resid, samples, weights, flags, out,
-    own, cols, held, stage, landed, recv, own_recv, res_recv, send, res_send, fill, out_sem,
+    depth, scale, resid, samples, weights, flags, held,
+    own, cols, mate, stage, landed, recv, own_recv, res_recv, mate_recv, send, res_send, fill,
 ):
     b = lax.axis_index("blk")
     w = lax.axis_index("wide")
@@ -87,6 +87,7 @@
         return (zz * 2 + yy) * 2 + cc
 
     orders = [sorted((o for o in range(depth) if o != i), key=lambda o: (abs(o - i), o)) for i in range(depth)]
+    inner = pick([int(len(o) > 1 and abs(o[1] - i) == 1) for i, o in enumerate(orders)], z)
 
     def order(k):
         value = z
@@ -138,6 +139,12 @@
             (down, push(h, src, w, 0, 1, at(z - 1, y, c))),
             (None, push(h, src, w, 0, 2, at(z, 1 - y, c))),
             (None, push(h, src, w, 0, 3, at(z, y, 1 - c))),
+        )
+
+    def mate_push(h):
+        return pltpu.make_async_remote_copy(
+            src_ref=own.at[h, nb], dst_ref=mate.at[h], send_sem=send.at[h, 0, 5],
+            recv_sem=mate_recv.at[h], device_id={"wide": at(z, y, 1 - c)}, device_id_type=MESH,
         )
 
     def z_pushes(h, k):
@@ -186,12 +193,6 @@
         return pltpu.make_async_remote_copy(
             src_ref=stage.at[panel], dst_ref=landed.at[panel], send_sem=res_send.at[panel],
             recv_sem=res_recv.at[panel], device_id={"blk": nb}, device_id_type=MESH,
-        )
-
-    def store(p, panel):
-        span = pl.ds(panel * per, per)
-        return pltpu.make_async_copy(
-            held.at[:, p, span], out.at[:, p, span], out_sem.at[p, panel]
         )
 
     def gram(p, side):
@@ -226,13 +227,13 @@
                     updated = jnp.where(on_diag, stepped, updated)
                 flag = flags[2 * t + p, slot].astype(jnp.float32)
                 held[t, p, slot] = updated * flag
-        store(p, panel).start()
 
     for load in loads:
         load.wait()
     for i in range(2):
         swap(i).start()
     start(own_pushes(b))
+    mate_push(b).start()
     swap_in = [
         pltpu.make_async_remote_copy(
             src_ref=own.at[nb, p], dst_ref=own.at[nb, p], send_sem=res_send.at[panels + i],
@@ -244,12 +245,6 @@
     start(own_pushes(nb))
     swap_in[1].wait_recv()
     forward_z(1)
-    load_weights.wait()
-
-    for p in range(2):
-        parity = b if p == 0 else nb
-        total = gram(p, lambda h, a: own[h, parity, a])
-        finish(p, w, lambda t, u: total[t * tile:(t + 1) * tile, u * tile:(u + 1) * tile], True)
 
     def place(s):
         k, i = s // 4, s % 4
@@ -257,12 +252,16 @@
         cc = jnp.where(i % 2 == 0, c, 1 - c)
         return k, i, at(order(k), yy, cc)
 
+    def cut(total):
+        return lambda t, u: total[t * tile:(t + 1) * tile, u * tile:(u + 1) * tile]
+
     def compute(s, carry):
         k, i, panel = place(s)
-
-        @pl.when(jnp.logical_and(i == 2, jnp.logical_and(k > 0, k < depth - 1)))
+        ahead = k + 1 + inner
+
+        @pl.when(jnp.logical_and(i == 2, jnp.logical_and(ahead > 1, ahead < depth)))
         def _():
-            forward_z(k + 1)
+            forward_z(ahead)
 
         @pl.when(i != 0)
         def _():
@@ -274,16 +273,31 @@
             for h in (b, nb):
                 start(y_push(h, k))
 
-        total = gram(1, lambda h, a: cols[h, panel, a])
+        total = cut(gram(1, lambda h, a: cols[h, panel, a]))
         for t in range(per):
             for u in range(per):
-                stage[panel, t, u] = total[t * tile:(t + 1) * tile, u * tile:(u + 1) * tile]
+                stage[panel, t, u] = total(t, u)
         hand(panel).start()
-        kept = gram(0, lambda h, a: cols[h, panel, a])
-        finish(0, panel, lambda t, u: kept[t * tile:(t + 1) * tile, u * tile:(u + 1) * tile], False)
+
+        @pl.when(s == 2)
+        def _():
+            mate_push(nb).start()
+            load_weights.wait()
+
+        finish(0, panel, cut(gram(0, lambda h, a: cols[h, panel, a])), False)
         return carry
 
-    lax.fori_loop(1, 4 * depth, compute, 0)
+    lax.fori_loop(2, 4 * depth, compute, 0)
+
+    for p in range(2):
+        parity = b if p == 0 else nb
+        finish(p, w, cut(gram(p, lambda h, a: own[h, parity, a])), True)
+    beside = at(z, y, 1 - c)
+    for h in (b, nb):
+        arrive(h, beside)
+        mate_push(h).wait_recv()
+    finish(0, beside, cut(gram(0, lambda h, a: cols[h, beside, a])), False)
+    finish(1, beside, cut(gram(1, lambda h, a: mate[h, a])), False)
 
     def receive(s, carry):
         panel = place(s)[2]
@@ -291,12 +305,13 @@
         finish(1, panel, lambda t, u: landed[panel, t, u], False)
         return carry
 
-    lax.fori_loop(1, 4 * depth, receive, 0)
+    lax.fori_loop(2, 4 * depth, receive, 0)
 
     for i in range(2):
         swap(i).wait_send()
     for h in (b, nb):
         drain(own_pushes(h))
+        mate_push(h).wait_send()
 
     def drain_group(k, carry):
         for h in (b, nb):
@@ -310,15 +325,10 @@
     lax.fori_loop(0, depth, drain_group, 0)
 
     def drain_panel(s, carry):
-        panel = place(s)[2]
-        hand(panel).wait_send()
-        for p in range(2):
-            store(p, panel).wait()
+        hand(place(s)[2]).wait_send()
         return carry
 
-    lax.fori_loop(1, 4 * depth, drain_panel, 0)
-    for p in range(2):
-        store(p, w).wait()
+    lax.fori_loop(2, 4 * depth, drain_panel, 0)
 
 
 def ring(resid, samples, precision, active):
@@ -333,25 +343,25 @@
     dma = pltpu.SemaphoreType.DMA
     updated = pl.pallas_call(
         functools.partial(kernel, depth, scale),
-        out_shape=jax.ShapeDtypeStruct((per, 2, per_class, tile, tile), f32),
+        out_shape=pltpu.VMEM((per, 2, per_class, tile, tile), f32),
         in_specs=[any_spec, any_spec, any_spec, pl.BlockSpec(memory_space=pltpu.SMEM)],
-        out_specs=any_spec,
+        out_specs=pl.BlockSpec(memory_space=pltpu.VMEM),
         scratch_shapes=[
             pltpu.VMEM((2, 2, 2, per, tile, half), bf16),
             pltpu.VMEM((2, panels, 2, per, tile, half), bf16),
-            pltpu.VMEM((per, 2, per_class, tile, tile), f32),
+            pltpu.VMEM((2, 2, per, tile, half), bf16),
             pltpu.VMEM((panels, per, per, tile, tile), f32),
             pltpu.VMEM((panels, per, per, tile, tile), f32),
             dma((2, panels)),
             dma((2,)),
             dma((panels,)),
-            dma((2, depth, 5)),
+            dma((2,)),
+            dma((2, depth, 6)),
             dma((panels + 2,)),
             dma((5,)),
-            dma((2, panels)),
         ],
         compiler_params=pltpu.CompilerParams(
-            collective_id=0, has_side_effects=True, vmem_limit_bytes=60 * 1024 * 1024
+            collective_id=0, has_side_effects=True, vmem_limit_bytes=52 * 1024 * 1024
         ),
     )(
         resid.reshape(per, 2, tile, half),

time: 131 us -> 115 us (0.88)
  Pallas kernels: 123 us -> 112 us
  local copies, waits for them, and re-layouts: 7.89 us -> 3.4 us
    pallas_call x1, Pallas kernels: 123 us -> 112 us  [ring(): pl.pallas_call(functools.partial(kernel, depth, scale), out_shape=pltpu.V...]
    unnamed x1, local copies, waits for them, and re-layouts: 7.89 us -> 3.4 us
where the time goes in v2:
time: 115 us
  Pallas kernels  112 us (97%)
  local copies, waits for them, and re-layouts  3.4 us (3%)
    pallas_call x1, Pallas kernels, ring(): pl.pallas_call(functools.partial(kernel, depth, scale), out_shape=pltpu.V...  112 us
    unnamed x1, local copies, waits for them, and re-layouts  3.4 us

profile of v2, /device:TPU:0, one launch (start us, length us, event | category | flops | bytes accessed | tf_op | source)
XLA Modules:
  0.0 115.2 jit_solution(109426418468383272)
XLA Ops:
  0.0 111.8 %shard_map.46 = f32[2,2,32,128,128]{4,3,2,1,0:T(8,128)S(1)} custom-call(bf16[2,2,128,512]{3,2,1,0:T(8,128)(2,1)} %bitcast.9, bf16[2,2,128,512]{3,2,1,0:T(8,128)(2,1)} %bitcast.10, f32[2,2,32,128,128]{4,3,2,1,0:T(8,128)} %bitcast.8, s32[4,32]{1,0:T(4,128)} %bitcast.11), custom_call_target="tpu_custom_call" | custom-call | tf_op jit(solution)/shard_map/pallas_call | solution.py:344
  111.8 3.4 %copy.7 = f32[4,1,32,128,128]{4,3,2,1,0:T(8,128)} copy(f32[4,1,32,128,128]{4,3,2,1,0:T(8,128)S(1)} %bitcast.7) | data formatting | bytes 16777216

commit v3 on v2

v3 whole, which is shorter than its diff:
```python
import functools

import jax
import jax.numpy as jnp
from jax import lax
from jax.experimental import pallas as pl
from jax.experimental.pallas import tpu as pltpu
from jax.sharding import PartitionSpec as P

STEP = 1.0
LASSO = 0.1
RIDGE = 0.5


def local(resid, samples, precision, active):
    groups = lax.axis_size("blk")
    column_group = lax.axis_index("blk")
    panel_index = lax.axis_index("wide")
    row_tiles = precision.shape[0]
    per_class = precision.shape[2]
    tile_size = precision.shape[3]
    tiles = per_class * groups
    local_samples = resid.shape[1]
    total_samples = local_samples * groups
    own_rows = panel_index * row_tiles + jnp.arange(row_tiles, dtype=jnp.int32)
    first_column = (column_group - own_rows) % groups
    own_resid = resid.reshape(row_tiles, tile_size, local_samples)
    own_data = samples.reshape(row_tiles, tile_size, local_samples)
    all_resid, all_data = (
        lax.all_gather(resid, "wide", axis=0, tiled=True),
        lax.all_gather(samples, "wide", axis=0, tiled=True),
    )
    resid_tiles = all_resid.reshape(tiles, tile_size, local_samples)
    data_tiles = all_data.reshape(tiles, tile_size, local_samples)
    positions = jnp.arange(per_class * lax.axis_size("blk"), dtype=jnp.int32)
    classes = positions // per_class
    within = positions % per_class
    column_ids = (classes[:, None] - own_rows[None, :]) % groups + groups * within[:, None]
    forward = jnp.einsum(
        "kis,pkjs->pkij", own_resid, data_tiles[column_ids], preferred_element_type=jnp.float32
    )
    backward = jnp.einsum(
        "kis,pkjs->pkij", own_data, resid_tiles[column_ids], preferred_element_type=jnp.float32
    )
    summed = (
        lax.psum_scatter(0.5 * (forward + backward), "blk", scatter_dimension=0, tiled=True)
        / total_samples
    )
    precision_tiles = precision[:, 0]
    active_flags = active[:, 0].astype(jnp.float32)
    gradient_part = summed.transpose(1, 0, 2, 3)
    column_ids = first_column[:, None] + groups * jnp.arange(per_class, dtype=jnp.int32)[None, :]
    same_tile = column_ids == own_rows[:, None]
    identity = jnp.eye(tile_size, dtype=bool)
    on_diag = same_tile[:, :, None, None] & identity
    inverse = jnp.where(on_diag, 1.0 / jnp.where(on_diag, precision_tiles, 1.0), 0.0)
    stepped = precision_tiles - STEP * (gradient_part + RIDGE * precision_tiles - inverse)
    shrunk = jnp.sign(stepped) * jnp.maximum(jnp.abs(stepped) - STEP * LASSO, 0.0)
    updated = jnp.where(on_diag, stepped, shrunk) * active_flags[:, :, None, None]
    return updated[:, None]


MESH = pl.DeviceIdType.MESH


def pick(table, i):
    value = jnp.int32(table[0])
    for n in range(1, len(table)):
        value = jnp.where(i == n, jnp.int32(table[n]), value)
    return value


def kernel(
    depth, scale, resid, samples, weights, flags, held,
    own, cols, mate, stage, landed, recv, own_recv, res_recv, mate_recv, send, own_send, res_send,
    mate_send, fill,
):
    b = lax.axis_index("blk")
    w = lax.axis_index("wide")
    nb = 1 - b
    z, y, c = w // 4, (w // 2) % 2, w % 2
    per = own.shape[2]
    tile = own.shape[4]
    panels = cols.shape[1]
    up, down = (z + 1 < depth), (z > 0)
    last = depth - 1
    inner = jnp.where(up, 1, 0) * jnp.where(down, 1, 0)
    far = jnp.where(2 * z < depth, 1, 0)
    far_z = far * last

    def at(zz, yy, cc):
        return (zz * 2 + yy) * 2 + cc

    orders = [
        sorted((o for o in range(depth) if o != i), key=lambda o: (abs(o - i), o))
        for i in range(depth)
    ]

    def order(k):
        value = z
        for n in range(1, depth):
            value = jnp.where(k == n, pick([orders[i][n - 1] for i in range(depth)], z), value)
        return value

    loads = []
    for a, src in enumerate((resid, samples)):
        for p in range(2):
            loads.append(
                pltpu.make_async_copy(src.at[:, p], own.at[b, p, :, a], fill.at[2 * a + p])
            )
    for load in loads:
        load.start()
    load_weights = pltpu.make_async_copy(weights, held, fill.at[4])

    barrier = pltpu.get_barrier_semaphore()

    def greet(**device):
        pl.semaphore_signal(barrier, inc=1, device_id=device, device_id_type=MESH)

    greet(blk=nb)
    greet(wide=at(z, 1 - y, c))
    greet(wide=at(z, y, 1 - c))

    @pl.when(up)
    def _():
        greet(wide=at(z + 1, y, c))

    @pl.when(down)
    def _():
        greet(wide=at(z - 1, y, c))

    pl.semaphore_wait(barrier, 3 + jnp.where(up, 1, 0) + jnp.where(down, 1, 0))

    def push(h, t, src, panel, k, lane, target):
        return pltpu.make_async_remote_copy(
            src_ref=src, dst_ref=cols.at[h, panel, t], send_sem=send.at[h, t, k, lane],
            recv_sem=recv.at[h, panel, t], device_id={"wide": target}, device_id_type=MESH,
        )

    def arrive(h, t, panel):
        push(h, t, cols.at[h, panel, t], panel, 0, 0, at(z, 1 - y, c)).wait_recv()

    def own_pushes(h, t):
        src = own.at[h, b, t]
        return (
            (up, push(h, t, src, w, 0, 0, at(z + 1, y, c))),
            (down, push(h, t, src, w, 0, 1, at(z - 1, y, c))),
            (None, push(h, t, src, w, 0, 2, at(z, 1 - y, c))),
            (None, push(h, t, src, w, 0, 3, at(z, y, 1 - c))),
        )

    def z_pushes(h, t, k):
        zk = order(k)
        panel = at(zk, y, c)
        src = cols.at[h, panel, t]
        onward = jnp.where(zk < z, z + 1, z - 1)
        exists = jnp.logical_and(onward >= 0, onward < depth)
        return (
            (exists, push(h, t, src, panel, k, 0, at(onward, y, c))),
            (None, push(h, t, src, panel, k, 2, at(z, 1 - y, c))),
            (None, push(h, t, src, panel, k, 3, at(z, y, 1 - c))),
        )

    def y_push(h, t, k):
        panel = at(order(k), 1 - y, c)
        return ((None, push(h, t, cols.at[h, panel, t], panel, k, 4, at(z, y, 1 - c))),)

    def mate_push(h, src, slot, lane, target):
        return pltpu.make_async_remote_copy(
            src_ref=src, dst_ref=mate.at[h, slot], send_sem=mate_send.at[h, lane],
            recv_sem=mate_recv.at[h, slot], device_id={"wide": target}, device_id_type=MESH,
        )

    def beside_push(h):
        return ((None, mate_push(h, own.at[h, nb], 0, 0, at(z, y, 1 - c))),)

    def end_push(h):
        slot = jnp.where(z == 0, 1, 2)
        inward = jnp.where(z == 0, z + 1, z - 1)
        return ((inner == 0, mate_push(h, own.at[h, nb], slot, 1, at(inward, y, c))),)

    def relay_push(h, end, lane):
        onward = jnp.where(end == 0, z + 1, z - 1)
        return ((inner == 1, mate_push(h, mate.at[h, 1 + end], 1 + end, lane, at(onward, y, c))),)

    def far_push(h):
        return ((None, mate_push(h, mate.at[h, 1 + far], 3, 4, at(z, y, 1 - c))),)

    def mate_arrive(h, slot):
        mate_push(h, mate.at[h, slot], slot, 0, at(z, y, 1 - c)).wait_recv()

    def start(pushes):
        for when, copy in pushes:
            if when is None:
                copy.start()
            else:
                pl.when(when)(copy.start)

    def drain(pushes):
        for when, copy in pushes:
            if when is None:
                copy.wait_send()
            else:
                pl.when(when)(copy.wait_send)

    def forward_z(k):
        for t in range(per):
            for h in (b, nb):
                arrive(h, t, at(order(k), y, c))
                start(z_pushes(h, t, k))

    def relay_near(h):
        @pl.when(inner == 1)
        def _():
            mate_arrive(h, 2 - far)
            start(relay_push(h, 1 - far, 2))

    def relay_far(h):
        mate_arrive(h, 1 + far)
        start(relay_push(h, far, 3))
        start(far_push(h))

    def swap(h, i, t):
        p = (nb, b)[i] if h is b else (b, nb)[i]
        return pltpu.make_async_remote_copy(
            src_ref=own.at[h, p, t], dst_ref=own.at[h, p, t], send_sem=own_send.at[i, t],
            recv_sem=own_recv.at[i, t], device_id={"blk": nb}, device_id_type=MESH,
        )

    def hand(panel, u):
        return pltpu.make_async_remote_copy(
            src_ref=stage.at[panel, u], dst_ref=landed.at[panel, u],
            send_sem=res_send.at[panel, u], recv_sem=res_recv.at[panel, u],
            device_id={"blk": nb}, device_id_type=MESH,
        )

    def gram(p, side):
        total = None
        for h in range(2):
            for a in range(2):
                left = own[h, p, :, a].reshape(per * tile, -1)
                right = side(h, 1 - a)
                part = lax.dot_general(
                    left, right, (((1,), (1,)), ((), ())), preferred_element_type=jnp.float32
                )
                total = part if total is None else total + part
        return total * scale

    def finish(p, panel, u, part, diagonal):
        for t in range(per):
            slot = panel * per + u
            weight = held[t, p, slot]
            half = part(t) + RIDGE * weight
            if diagonal and t == u:
                rows = lax.broadcasted_iota(jnp.int32, (tile, tile), 0)
                columns = lax.broadcasted_iota(jnp.int32, (tile, tile), 1)
                on_diag = rows == columns + b * (2 * tile)
                inverse = jnp.where(on_diag, 1.0 / jnp.where(on_diag, weight, 1.0), 0.0)
                stepped = weight - STEP * (half - inverse)
            else:
                stepped = weight - STEP * half
            bound = STEP * LASSO
            updated = stepped - jnp.clip(stepped, -bound, bound)
            if diagonal and t == u:
                updated = jnp.where(on_diag, stepped, updated)
            flag = flags[2 * t + p, slot].astype(jnp.float32)
            held[t, p, slot] = updated * flag

    def cut(total):
        return lambda t: total[t * tile:(t + 1) * tile]

    for load in loads:
        load.wait()
    for i in range(2):
        for t in range(per):
            swap(b, i, t).start()
    for t in range(per):
        start(own_pushes(b, t))
    load_weights.start()
    for t in range(per):
        swap(nb, 0, t).wait_recv()
        start(own_pushes(nb, t))
    start(end_push(b))
    start(beside_push(b))
    for h in (b, nb):
        for t in range(per):
            arrive(h, t, at(order(1), y, c))
            start(z_pushes(h, t, 1))
    for t in range(per):
        swap(nb, 1, t).wait_recv()
    start(end_push(nb))
    load_weights.wait()

    def place(n):
        s = n + 2 + jnp.where(n < 4 * depth - 6, 0, 2)
        k, i = s // 4, s % 4
        yy = jnp.where(i < 2, y, 1 - y)
        cc = jnp.where(i % 2 == 0, c, 1 - c)
        return k, i, at(order(k), yy, cc)

    steps = 4 * depth - 4
    middle = steps // 2

    def receive(n, carry):
        panel = place(n)[2]
        for u in range(per):
            hand(panel, u).wait_recv()
            finish(1, panel, u, lambda t: landed[panel, u, t], False)
        return carry

    def nearby():
        for u in range(per):
            for p in range(2):
                parity = b if p == 0 else nb
                finish(p, w, u, cut(gram(p, lambda h, a: own[h, parity, u, a])), True)
        panel = at(z, y, 1 - c)
        for h in (b, nb):
            for t in range(per):
                arrive(h, t, panel)
            mate_arrive(h, 0)
        for u in range(per):
            finish(0, panel, u, cut(gram(0, lambda h, a: cols[h, panel, u, a])), False)
            finish(1, panel, u, cut(gram(1, lambda h, a: mate[h, 0, u, a])), False)

    def compute(n, carry):
        k, i, panel = place(n)
        ahead = k + 1 + inner

        @pl.when(jnp.logical_and(i == 2, k == 1))
        def _():
            nearby()

        @pl.when(jnp.logical_and(i == 2, jnp.logical_and(ahead > 1, ahead < depth)))
        def _():
            forward_z(ahead)

        @pl.when(jnp.logical_and(i == 2, k == 1))
        def _():
            relay_near(b)

        @pl.when(jnp.logical_and(i == 2, jnp.logical_and(k == 2, inner == 1)))
        def _():
            relay_far(b)

        @pl.when(jnp.logical_and(i == 2, k == last))
        def _():
            lax.fori_loop(0, middle, receive, 0)

        for u in range(per):
            @pl.when(i != 0)
            def _():
                for h in (b, nb):
                    arrive(h, u, panel)

            @pl.when(i == 2)
            def _():
                for h in (b, nb):
                    start(y_push(h, u, k))

            total = cut(gram(1, lambda h, a: cols[h, panel, u, a]))
            for t in range(per):
                stage[panel, u, t] = total(t)
            hand(panel, u).start()

        @pl.when(n == 0)
        def _():
            start(beside_push(nb))

        for u in range(per):
            finish(0, panel, u, cut(gram(0, lambda h, a: cols[h, panel, u, a])), False)

        @pl.when(jnp.logical_and(i == 3, k == 1))
        def _():
            relay_near(nb)

        @pl.when(jnp.logical_and(i == 3, jnp.logical_and(k == 2, inner == 1)))
        def _():
            relay_far(nb)

        return carry

    lax.fori_loop(0, steps, compute, 0)

    @pl.when(inner == 0)
    def _():
        for h in (b, nb):
            relay_far(h)

    def distant(n, carry):
        cc = jnp.where(n == 0, c, 1 - c)
        slot = jnp.where(n == 0, 1 + far, 3)
        panel = at(far_z, y, cc)

        @pl.when(n == 1)
        def _():
            for h in (b, nb):
                for t in range(per):
                    arrive(h, t, panel)
                mate_arrive(h, 3)

        for u in range(per):
            finish(0, panel, u, cut(gram(0, lambda h, a: cols[h, panel, u, a])), False)
            finish(1, panel, u, cut(gram(1, lambda h, a: mate[h, slot, u, a])), False)
        return carry

    lax.fori_loop(0, 2, distant, 0)
    lax.fori_loop(middle, steps, receive, 0)

    for i in range(2):
        for t in range(per):
            swap(b, i, t).wait_send()
    for h in (b, nb):
        for t in range(per):
            drain(own_pushes(h, t))
        drain(beside_push(h))
        drain(end_push(h))
        drain(relay_push(h, 1 - far, 2))
        drain(relay_push(h, far, 3))
        drain(far_push(h))

    def drain_group(k, carry):
        for h in (b, nb):
            for t in range(per):
                drain(y_push(h, t, k))

                @pl.when(k > 0)
                def _():
                    drain(z_pushes(h, t, k))
        return carry

    lax.fori_loop(0, depth, drain_group, 0)

    def drain_panel(n, carry):
        for u in range(per):
            hand(place(n)[2], u).wait_send()
        return carry

    lax.fori_loop(0, steps, drain_panel, 0)


def ring(resid, samples, precision, active):
    panels = lax.axis_size("wide")
    row_tiles, _, per_class, tile, _ = precision.shape
    per = row_tiles // 2
    half = resid.shape[1]
    depth = panels // 4
    scale = 0.5 / (2 * half)
    any_spec = pl.BlockSpec(memory_space=pl.ANY)
    bf16, f32 = resid.dtype, jnp.float32
    dma = pltpu.SemaphoreType.DMA
    updated = pl.pallas_call(
        functools.partial(kernel, depth, scale),
        out_shape=pltpu.VMEM((per, 2, per_class, tile, tile), f32),
        in_specs=[any_spec, any_spec, any_spec, pl.BlockSpec(memory_space=pltpu.SMEM)],
        out_specs=pl.BlockSpec(memory_space=pltpu.VMEM),
        scratch_shapes=[
            pltpu.VMEM((2, 2, per, 2, tile, half), bf16),
            pltpu.VMEM((2, panels, per, 2, tile, half), bf16),
            pltpu.VMEM((2, 4, per, 2, tile, half), bf16),
            pltpu.VMEM((panels, per, per, tile, tile), f32),
            pltpu.VMEM((panels, per, per, tile, tile), f32),
            dma((2, panels, per)),
            dma((2, per)),
            dma((panels, per)),
            dma((2, 4)),
            dma((2, per, depth, 5)),
            dma((2, per)),
            dma((panels, per)),
            dma((2, 5)),
            dma((5,)),
        ],
        compiler_params=pltpu.CompilerParams(
            collective_id=0, has_side_effects=True, vmem_limit_bytes=52 * 1024 * 1024
        ),
    )(
        resid.reshape(per, 2, tile, half),
        samples.reshape(per, 2, tile, half),
        precision.reshape(per, 2, per_class, tile, tile),
        active[:, 0],
    )
    return updated.reshape(precision.shape)


def body(resid, samples, precision, active):
    panels = lax.axis_size("wide")
    row_tiles, _, per_class, tile, _ = precision.shape
    words = 8 * per_class * row_tiles * tile * tile + 4 * panels * row_tiles * tile * resid.shape[1]
    if lax.axis_size("blk") == 2 and panels // 4 == 4 and row_tiles % 2 == 0 and words < 52 * 1024 * 1024:
        return ring(resid, samples, precision, active)
    return local(resid, samples, precision, active)


def solution(mesh):
    in_specs = (
        P("wide", "blk"),
        P("wide", "blk"),
        P("wide", "blk", None, None, None),
        P("wide", "blk", None),
    )
    out_specs = P("wide", "blk", None, None, None)
    return jax.shard_map(body, mesh=mesh, in_specs=in_specs, out_specs=out_specs, check_vma=False)
```

time: 115 us -> 112 us (0.974)
  Pallas kernels: 112 us -> 109 us
    pallas_call x1, Pallas kernels: 112 us -> 109 us  [ring(): pl.pallas_call(functools.partial(kernel, depth, scale), out_shape=pltpu.V...]
where the time goes in v3:
time: 112 us
  Pallas kernels  109 us (97%)
  local copies, waits for them, and re-layouts  3.4 us (3%)
    pallas_call x1, Pallas kernels, ring(): pl.pallas_call(functools.partial(kernel, depth, scale), out_shape=pltpu.V...  109 us
    unnamed x1, local copies, waits for them, and re-layouts  3.4 us

profile of v3, /device:TPU:0, one launch (start us, length us, event | category | flops | bytes accessed | tf_op | source)
XLA Modules:
  0.0 112.2 jit_solution(1263063674913102093)
XLA Ops:
  0.0 108.8 %shard_map.46 = f32[2,2,32,128,128]{4,3,2,1,0:T(8,128)S(1)} custom-call(bf16[2,2,128,512]{3,2,1,0:T(8,128)(2,1)} %bitcast.9, bf16[2,2,128,512]{3,2,1,0:T(8,128)(2,1)} %bitcast.10, f32[2,2,32,128,128]{4,3,2,1,0:T(8,128)} %bitcast.8, s32[4,32]{1,0:T(4,128)} %bitcast.11), custom_call_target="tpu_custom_call" | custom-call | tf_op jit(solution)/shard_map/pallas_call | solution.py:451
  108.8 3.4 %copy.7 = f32[4,1,32,128,128]{4,3,2,1,0:T(8,128)} copy(f32[4,1,32,128,128]{4,3,2,1,0:T(8,128)S(1)} %bitcast.7) | data formatting | bytes 16777216

commit v4 on v3

--- a/solution.py
+++ b/solution.py
@@ -239,7 +239,7 @@
         for h in range(2):
             for a in range(2):
                 left = own[h, p, :, a].reshape(per * tile, -1)
-                right = side(h, 1 - a)
+                right = side(h, 1 - a).reshape(-1, own.shape[5])
                 part = lax.dot_general(
                     left, right, (((1,), (1,)), ((), ())), preferred_element_type=jnp.float32
                 )
@@ -266,8 +266,12 @@
             flag = flags[2 * t + p, slot].astype(jnp.float32)
             held[t, p, slot] = updated * flag
 
-    def cut(total):
-        return lambda t: total[t * tile:(t + 1) * tile]
+    def cut(total, u=0):
+        return lambda t: total[t * tile:(t + 1) * tile, u * tile:(u + 1) * tile]
+
+    def finish_all(p, panel, total, diagonal):
+        for u in range(per):
+            finish(p, panel, u, cut(total, u), diagonal)
 
     for load in loads:
         load.wait()
@@ -286,6 +290,11 @@
         for t in range(per):
             arrive(h, t, at(order(1), y, c))
             start(z_pushes(h, t, 1))
+
+            @pl.when(inner == 1)
+            def _():
+                arrive(h, t, at(order(2), y, c))
+                start(z_pushes(h, t, 2))
     for t in range(per):
         swap(nb, 1, t).wait_recv()
     start(end_push(nb))
@@ -299,7 +308,7 @@
         return k, i, at(order(k), yy, cc)
 
     steps = 4 * depth - 4
-    middle = steps // 2
+    middle = steps - 4
 
     def receive(n, carry):
         panel = place(n)[2]
@@ -308,19 +317,20 @@
             finish(1, panel, u, lambda t: landed[panel, u, t], False)
         return carry
 
+    def keep(panel):
+        finish_all(0, panel, gram(0, lambda h, a: cols[h, panel, :, a]), False)
+
     def nearby():
-        for u in range(per):
-            for p in range(2):
-                parity = b if p == 0 else nb
-                finish(p, w, u, cut(gram(p, lambda h, a: own[h, parity, u, a])), True)
+        for p in range(2):
+            parity = b if p == 0 else nb
+            finish_all(p, w, gram(p, lambda h, a: own[h, parity, :, a]), True)
         panel = at(z, y, 1 - c)
         for h in (b, nb):
             for t in range(per):
                 arrive(h, t, panel)
             mate_arrive(h, 0)
-        for u in range(per):
-            finish(0, panel, u, cut(gram(0, lambda h, a: cols[h, panel, u, a])), False)
-            finish(1, panel, u, cut(gram(1, lambda h, a: mate[h, 0, u, a])), False)
+        keep(panel)
+        finish_all(1, panel, gram(1, lambda h, a: mate[h, 0, :, a]), False)
 
     def compute(n, carry):
         k, i, panel = place(n)
@@ -330,7 +340,7 @@
         def _():
             nearby()
 
-        @pl.when(jnp.logical_and(i == 2, jnp.logical_and(ahead > 1, ahead < depth)))
+        @pl.when(jnp.logical_and(i == 2, jnp.logical_and(k > 0, ahead < depth)))
         def _():
             forward_z(ahead)
 
@@ -366,8 +376,9 @@
         def _():
             start(beside_push(nb))
 
-        for u in range(per):
-            finish(0, panel, u, cut(gram(0, lambda h, a: cols[h, panel, u, a])), False)
+        @pl.when(k < last)
+        def _():
+            keep(panel)
 
         @pl.when(jnp.logical_and(i == 3, k == 1))
         def _():
@@ -380,6 +391,12 @@
         return carry
 
     lax.fori_loop(0, steps, compute, 0)
+
+    def keep_late(n, carry):
+        keep(place(n)[2])
+        return carry
+
+    lax.fori_loop(steps - 2, steps, keep_late, 0)
 
     @pl.when(inner == 0)
     def _():
@@ -398,9 +415,8 @@
                     arrive(h, t, panel)
                 mate_arrive(h, 3)
 
-        for u in range(per):
-            finish(0, panel, u, cut(gram(0, lambda h, a: cols[h, panel, u, a])), False)
-            finish(1, panel, u, cut(gram(1, lambda h, a: mate[h, slot, u, a])), False)
+        keep(panel)
+        finish_all(1, panel, gram(1, lambda h, a: mate[h, slot, :, a]), False)
         return carry
 
     lax.fori_loop(0, 2, distant, 0)

time: 112 us -> 116 us (1.036)
  the two profiles are of different devices: /device:TPU:0 before, /device:TPU:8 now
where the time goes in v4:
time: 116 us
  Pallas kernels  113 us (97%)
  local copies, waits for them, and re-layouts  3.4 us (3%)
    pallas_call x1, Pallas kernels, ring(): pl.pallas_call(functools.partial(kernel, depth, scale), out_shape=pltpu.V...  113 us
    unnamed x1, local copies, waits for them, and re-layouts  3.4 us

profile of v4, /device:TPU:8, one launch (start us, length us, event | category | flops | bytes accessed | tf_op | source)
XLA Modules:
  0.0 116.3 jit_solution(6012267793213748637)
XLA Ops:
  0.0 112.9 %shard_map.46 = f32[2,2,32,128,128]{4,3,2,1,0:T(8,128)S(1)} custom-call(bf16[2,2,128,512]{3,2,1,0:T(8,128)(2,1)} %bitcast.9, bf16[2,2,128,512]{3,2,1,0:T(8,128)(2,1)} %bitcast.10, f32[2,2,32,128,128]{4,3,2,1,0:T(8,128)} %bitcast.8, s32[4,32]{1,0:T(4,128)} %bitcast.11), custom_call_target="tpu_custom_call" | custom-call | tf_op jit(solution)/shard_map/pallas_call | solution.py:467
  112.9 3.4 %copy.7 = f32[4,1,32,128,128]{4,3,2,1,0:T(8,128)} copy(f32[4,1,32,128,128]{4,3,2,1,0:T(8,128)S(1)} %bitcast.7) | data formatting | bytes 16777216

commit v5 on v4

--- a/solution.py
+++ b/solution.py
@@ -294,7 +294,7 @@
             @pl.when(inner == 1)
             def _():
                 arrive(h, t, at(order(2), y, c))
-                start(z_pushes(h, t, 2))
+                start(z_pushes(h, t, 2)[:1])
     for t in range(per):
         swap(nb, 1, t).wait_recv()
     start(end_push(nb))
@@ -339,6 +339,12 @@
         @pl.when(jnp.logical_and(i == 2, k == 1))
         def _():
             nearby()
+
+        @pl.when(jnp.logical_and(n == 0, inner == 1))
+        def _():
+            for t in range(per):
+                for h in (b, nb):
+                    start(z_pushes(h, t, 2)[1:])
 
         @pl.when(jnp.logical_and(i == 2, jnp.logical_and(k > 0, ahead < depth)))
         def _():

time: 116 us -> 112 us (0.966)
  the two profiles are of different devices: /device:TPU:8 before, /device:TPU:0 now
where the time goes in v5:
time: 112 us
  Pallas kernels  109 us (97%)
  local copies, waits for them, and re-layouts  3.4 us (3%)
    pallas_call x1, Pallas kernels, ring(): pl.pallas_call(functools.partial(kernel, depth, scale), out_shape=pltpu.V...  109 us
    unnamed x1, local copies, waits for them, and re-layouts  3.4 us

profile of v5, /device:TPU:0, one launch (start us, length us, event | category | flops | bytes accessed | tf_op | source)
XLA Modules:
  0.0 112.1 jit_solution(4696923918709145215)
XLA Ops:
  0.0 108.7 %shard_map.46 = f32[2,2,32,128,128]{4,3,2,1,0:T(8,128)S(1)} custom-call(bf16[2,2,128,512]{3,2,1,0:T(8,128)(2,1)} %bitcast.9, bf16[2,2,128,512]{3,2,1,0:T(8,128)(2,1)} %bitcast.10, f32[2,2,32,128,128]{4,3,2,1,0:T(8,128)} %bitcast.8, s32[4,32]{1,0:T(4,128)} %bitcast.11), custom_call_target="tpu_custom_call" | custom-call | tf_op jit(solution)/shard_map/pallas_call | solution.py:473
  108.7 3.4 %copy.7 = f32[4,1,32,128,128]{4,3,2,1,0:T(8,128)} copy(f32[4,1,32,128,128]{4,3,2,1,0:T(8,128)S(1)} %bitcast.7) | data formatting | bytes 16777216

commit v6 on v5

--- a/solution.py
+++ b/solution.py
@@ -354,7 +354,7 @@
         def _():
             relay_near(b)
 
-        @pl.when(jnp.logical_and(i == 2, jnp.logical_and(k == 2, inner == 1)))
+        @pl.when(jnp.logical_and(i == 2, k == last - inner))
         def _():
             relay_far(b)
 
@@ -406,8 +406,7 @@
 
     @pl.when(inner == 0)
     def _():
-        for h in (b, nb):
-            relay_far(h)
+        relay_far(nb)
 
     def distant(n, carry):
         cc = jnp.where(n == 0, c, 1 - c)

time: 112 us -> 112 us (level)
  no operation moved by 1% of the time
where the time goes in v6:
time: 112 us
  Pallas kernels  109 us (97%)
  local copies, waits for them, and re-layouts  3.4 us (3%)
    pallas_call x1, Pallas kernels, ring(): pl.pallas_call(functools.partial(kernel, depth, scale), out_shape=pltpu.V...  109 us
    unnamed x1, local copies, waits for them, and re-layouts  3.4 us

profile of v6, /device:TPU:0, one launch (start us, length us, event | category | flops | bytes accessed | tf_op | source)
XLA Modules:
  0.0 112.1 jit_solution(17689262707071848275)
XLA Ops:
  0.0 108.7 %shard_map.46 = f32[2,2,32,128,128]{4,3,2,1,0:T(8,128)S(1)} custom-call(bf16[2,2,128,512]{3,2,1,0:T(8,128)(2,1)} %bitcast.9, bf16[2,2,128,512]{3,2,1,0:T(8,128)(2,1)} %bitcast.10, f32[2,2,32,128,128]{4,3,2,1,0:T(8,128)} %bitcast.8, s32[4,32]{1,0:T(4,128)} %bitcast.11), custom_call_target="tpu_custom_call" | custom-call | tf_op jit(solution)/shard_map/pallas_call | solution.py:472
  108.7 3.4 %copy.7 = f32[4,1,32,128,128]{4,3,2,1,0:T(8,128)} copy(f32[4,1,32,128,128]{4,3,2,1,0:T(8,128)S(1)} %bitcast.7) | data formatting | bytes 16777216
